TPU v7x, 32 devices: a whole 2x2x4 slice. The times are simulated.
32 devices in a mesh: row: 8 (over z, core), col: 4 (over y, x).
Axes of the slice: x: 2, y: 2, z: 4, core: 2. Of those that a mesh axis runs over, the one named last changes fastest.
Arguments:
- matrix: float32 [8192, 4096], P('row', 'col'), may hold values from -6 to 166
Outputs:
- updated: float32 [8192, 4096], P('row', 'col')
All inputs are finite; a program needn't handle non-finite values.
Results may differ from a plain program's by a relative error of at most 0.0003.
Values sent between devices are 32-bit elements; how exact they have to be, the bound alone decides.
No kernel may reach another device: no remote copies, remote signals or barrier semaphores. Data moves between devices by JAX's collectives and lax.ppermute only.
A program may use at most 64 MiB of HBM per device.

v0:
```python
import jax
import jax.numpy as jnp
from jax import lax
from jax.sharding import PartitionSpec as P

NB = 128


def from_root(value, axis, source):
    kept = jnp.where(lax.axis_index(axis) == source, value, 0).astype(value.dtype)
    return lax.psum(kept, axis)


def factor(corner):
    symmetric = jnp.tril(corner) + jnp.tril(corner, -1).T
    lower_factor = jnp.linalg.cholesky(symmetric)
    identity = jnp.eye(corner.shape[0], dtype=jnp.float32)
    inverse = jax.scipy.linalg.solve_triangular(lower_factor, identity, lower=True)
    return (lower_factor, inverse)


def body(matrix):
    rows_here = lax.axis_size("row")
    cols_here = lax.axis_size("col")
    row_index = lax.axis_index("row")
    col_index = lax.axis_index("col")
    row_blocks = matrix.shape[0] // NB
    col_blocks = matrix.shape[1] // NB
    corner = matrix[:NB, :NB]
    local_factor, local_inverse = factor(corner)
    stacked = from_root(jnp.stack([local_factor, local_inverse]), "row", 0)
    lower_factor = stacked[0]
    inverse = stacked[1]
    panel = lax.dot_general(
        matrix[:, :NB],
        inverse,
        (((1,), (1,)), ((), ())),
        precision=lax.Precision.HIGHEST,
        preferred_element_type=jnp.float32,
    )
    panel = panel.at[:NB].set(jnp.where(row_index == 0, lower_factor, panel[:NB]))
    panel = from_root(panel, "col", 0)
    whole = lax.all_gather(panel, "row", axis=0, tiled=True)
    all_blocks = whole.reshape(rows_here * row_blocks, NB, NB)
    wanted = jnp.arange(col_blocks, dtype=jnp.int32) * cols_here + col_index
    source_rows = wanted % rows_here * row_blocks + wanted // rows_here
    mirror = jnp.take(all_blocks, source_rows, axis=0).reshape(col_blocks * NB, NB)
    product = lax.dot_general(
        panel,
        mirror,
        (((1,), (1,)), ((), ())),
        precision=lax.Precision.HIGHEST,
        preferred_element_type=jnp.float32,
    )
    fresh = matrix - product
    global_rows = jnp.arange(row_blocks, dtype=jnp.int32) * rows_here + row_index
    global_cols = jnp.arange(col_blocks, dtype=jnp.int32) * cols_here + col_index
    keep_mask = (global_rows[:, None] >= global_cols[None, :]) & (global_cols[None, :] >= 1)
    shaped_old = matrix.reshape(row_blocks, NB, col_blocks, NB)
    shaped_new = fresh.reshape(row_blocks, NB, col_blocks, NB)
    result = jnp.where(keep_mask[:, None, :, None], shaped_new, shaped_old).reshape(matrix.shape)
    result = result.at[:, :NB].set(jnp.where(col_index == 0, panel, result[:, :NB]))
    return result


def solution(mesh):
    return jax.shard_map(
        body, mesh=mesh, in_specs=(P("row", "col"),), out_specs=P("row", "col"), check_vma=False
    )
```

profile of v0, /device:TPU:0, one launch (start us, length us, event | category | flops | bytes accessed | tf_op | source)
XLA Modules:
  0.0 205.8 jit_solution(1696970586358199093)
XLA Ops:
  6.5 0.0 all-reduce.3.cloned.1.call-start
  6.5 0.8 slice.64
  7.4 0.1 copy.8
  7.5 0.9 bitcast_add_fusion.1
  8.3 0.1 copy.5
  8.5 11.7 %cholesky.19 = f32[128,128]{1,0:T(8,128)S(1)} custom-call(f32[128,128]{1,0:T(8,128)S(1)} %fusion.4), custom_call_target="Cholesky" | custom-call | tf_op jit(solution)/shard_map/jit(cholesky)/cholesky | solution.py:16
  20.2 0.6 compare_reduce_fusion.1
  20.9 0.7 fusion.5
  21.5 9.8 %custom-call.7 = f32[1,128,128]{1,2,0:T(8,128)S(1)} custom-call(f32[1,128,128]{2,1,0:T(8,128)S(1)} %get-tuple-element.30), custom_call_target="InvertDiagBlocksLowerTriangular" | custom-call | tf_op jit(solution)/shard_map/jit(_solve_triangular)/triangular_solve | solution.py:18
  31.3 0.2 convolution_bitcast_fusion.1
  31.6 0.7 maximum_select_fusion
  32.3 0.0 all-reduce.3.cloned.1.call-update
  32.3 0.0 all-reduce.5.cloned.1.call-start
  32.3 57.0 %all-reduce.3.cloned.1.call-done = f32[2,128,128]{2,1,0:T(8,128)} async-done(((f32[2,128,128]{2,1,0:T(8,128)}), f32[2,128,128]{2,1,0:T(8,128)}) %all-reduce.3.cloned.1.call-update) | async-done | bytes 131088 | tf_op jit(solution)/shard_map/psum | solution.py:11
  89.3 1.7 convolution_bitcast_fusion
  91.0 0.9 fusion.2
  91.8 0.8 broadcast_select_fusion
  92.7 0.0 all-reduce.5.cloned.1.call-update
  92.7 0.0 all-gather.2.cloned.1.call-start
  92.8 44.4 %all-reduce.5.cloned.1.call-done = f32[1024,128]{1,0:T(8,128)} async-done(((f32[1024,128]{1,0:T(8,128)}), f32[1024,128]{1,0:T(8,128)}) %all-reduce.5.cloned.1.call-update) | async-done | bytes 524304 | tf_op jit(solution)/shard_map/psum | solution.py:11
  137.2 0.0 all-gather.2.cloned.1.call-update
  137.2 0.6 compare_reduce_fusion
  137.9 0.1 broadcast_bitcast_fusion
  138.0 0.1 compare_and_fusion
  138.1 48.0 %all-gather.2.cloned.1.call-done = f32[8192,128]{1,0:T(8,128)} async-done(((f32[1024,128]{1,0:T(8,128)}), f32[8192,128]{1,0:T(8,128)}) %all-gather.2.cloned.1.call-update) | async-done | bytes 4194320 | tf_op jit(solution)/shard_map/all_gather | solution.py:43
  186.1 2.8 %gather_fusion = f32[8,128,128]{2,1,0:T(8,128)S(1)} fusion(f32[64,128,128]{2,1,0:T(8,128)} %bitcast.38, s32[1024]{0:T(1024)S(1)} %pad_clamp_fusion), kind=kCustom, calls=%fused_computation | custom fusion | bytes 1048608 | tf_op jit(solution)/shard_map/jit(_take)/gather | solution.py:47
  188.8 0.2 bitcast_select_fusion
  189.0 0.3 broadcast_in_dim.44
  189.4 0.0 copy-start
  189.4 7.4 %subtract_select_fusion = f32[1024,1024]{1,0:T(8,128)} fusion(f32[1024,1024]{1,0:T(8,128)} %param.5, pred[128,8,8,128]{3,2,1,0:T(8,128)(4,1)S(1)} %bitcast.37, f32[1024,128]{1,0:T(8,128)} %all-reduce.5.cloned.1.call-done, f32[1024,128]{1,0:T(8,128)S(1)} %bitcast_select_fusion), kind=kOutput, calls=%fused_computation.1 | convolution fusion | flops 1612709888 | bytes 10485760 | tf_op jit(solution)/shard_map/dot_general | solution.py:48
  196.8 0.0 copy-done
  196.8 2.5 %fusion = f32[1024,1024]{1,0:T(8,128)} fusion(f32[1024,1024]{1,0:T(8,128)} %subtract_select_fusion, f32[1024,128]{1,0:T(8,128)S(1)} %copy-done, pred[]{:T(512)} %compare_reduce_fusion, pred[]{:T(512)S(6)} %eq.6), kind=kLoop, calls=%fused_computation.5 | loop fusion | flops 262144 | bytes 1573377 | tf_op jit(solution)/shard_map/scatter | solution.py:62
  (9 shorter events, 0.1 us)
Async XLA Ops:
  6.5 82.8 %all-reduce.3.cloned.1.call-start = ((), (), s32[]{:S(2)}) async-start(), calls=%async_computation | async-start | bytes 262144 | tf_op jit(solution)/shard_map/psum | solution.py:11
  32.3 104.9 %all-reduce.5.cloned.1.call-start = ((), (), s32[]{:S(2)}) async-start(), calls=%async_computation.1 | async-start | bytes 1048576 | tf_op jit(solution)/shard_map/psum | solution.py:11
  92.7 93.4 %all-gather.2.cloned.1.call-start = ((), (), s32[]{:S(2)}) async-start(), calls=%async_computation.2 | async-start | bytes 4718592 | tf_op jit(solution)/shard_map/all_gather | solution.py:43
  189.4 7.4 %copy-start = (f32[1024,128]{1,0:T(8,128)S(1)}, f32[1024,128]{1,0:T(8,128)}, u32[]{:S(2)}) copy-start(f32[1024,128]{1,0:T(8,128)} %all-reduce.5.cloned.1.call-done) | copy-start | bytes 1572868
Sparse Core Ops, SparseCore 0:
  32.4 56.8 all-reduce.2
  92.8 44.3 all-reduce.4
  138.9 47.1 all-gather.1
where the time goes:
time: 206 us
  waiting for transfers between devices  149 us (72%)
  other arithmetic  29.5 us (14%)
  between operations  13.2 us (6%)
  matrix products  9.34 us (5%)
  local copies, waits for them, and re-layouts  4.2 us (2%)
    psum x2, waiting for transfers between devices, from_root(): return lax.psum(kept, axis)  101 us
    all_gather x1, waiting for transfers between devices, body(): whole = lax.all_gather(panel, 'row', axis=0, tiled=True)  48 us
    another operation x3, other arithmetic, factor(): lower_factor = jnp.linalg.cholesky(symmetric)  12.4 us
    another operation x1, other arithmetic, factor(): jax.scipy.linalg.solve_triangular(lower_factor, identity, lower=True)  9.81 us
    dot_general x1, matrix products, body(): lax.dot_general(panel, mirror, (((1,), (1,)), ((), ())), precision=lax.Pr...  7.43 us
  transfers between devices with their start and end apart: 3, of which 3 were waited for; matrix products, arithmetic and copies ran while one was open for 0% of the time, Pallas kernels for 0%

commit v1 on v0

--- a/solution.py
+++ b/solution.py
@@ -40,7 +40,23 @@
     )
     panel = panel.at[:NB].set(jnp.where(row_index == 0, lower_factor, panel[:NB]))
     panel = from_root(panel, "col", 0)
-    whole = lax.all_gather(panel, "row", axis=0, tiled=True)
+    answer, oldest, v_now = (lax.psum(1, "row"), lax.axis_index("row"), panel.shape[0])
+    row_list = tuple(((idx, (idx + 1) % answer) for idx in range(answer)))
+    fields = tuple(((idx, (idx - 1) % answer) for idx in range(answer)))
+    whole = jnp.zeros((*panel.shape[:0], answer * v_now, *panel.shape[1:]), panel.dtype)
+    whole = lax.dynamic_update_slice_in_dim(whole, panel, oldest * v_now, axis=0)
+    y_new = earlier = panel
+    block_now = answer // 2
+    i = 1
+    while i < block_now + 1:
+        y_new = lax.ppermute(y_new, "row", row_list)
+        whole = lax.dynamic_update_slice_in_dim(whole, y_new, (oldest - i) % answer * v_now, axis=0)
+        if i < answer - block_now:
+            earlier = lax.ppermute(earlier, "row", fields)
+            whole = lax.dynamic_update_slice_in_dim(
+                whole, earlier, (oldest + i) % answer * v_now, axis=0
+            )
+        i += 1
     all_blocks = whole.reshape(rows_here * row_blocks, NB, NB)
     wanted = jnp.arange(col_blocks, dtype=jnp.int32) * cols_here + col_index
     source_rows = wanted % rows_here * row_blocks + wanted // rows_here

time: 206 us -> 214 us (1.039)
  waiting for transfers between devices: 149 us -> 138 us
  starting transfers between devices: 0.09 us -> 10.7 us
  local copies, waits for them, and re-layouts: 4.2 us -> 13.1 us
    all_gather x1 -> x0, waiting for transfers between devices: 48 us -> none  [body(): whole = lax.all_gather(panel, 'row', axis=0, tiled=True)]
    ppermute x0 -> x7, waiting for transfers between devices: none -> 36.7 us  [the longest x4 36.7 us: body(): y_new = lax.ppermute(y_new, 'row', row_list)]
    ppermute x0 -> x7, starting transfers between devices: none -> 10.7 us  [the longest x3 10.7 us: body(): earlier = lax.ppermute(earlier, 'row', fields)]
    dynamic_update_slice x0 -> x8, local copies, waits for them, and re-layouts: none -> 6.61 us  [the longest x4 3.31 us: body(): lax.dynamic_update_slice_in_dim(whole, y_new, (oldest - i) % answer * v_n...]
    broadcast_in_dim x0 -> x1, local copies, waits for them, and re-layouts: none -> 2.28 us  [body(): jnp.zeros((*panel.shape[:0], answer * v_now, *panel.shape[1:]), panel.dtype)]
  transfers between devices with their start and end apart: 3 -> 9, of which waited for: 3 -> 6; matrix products, arithmetic and copies ran while one was open for 0% -> 4% of each run, Pallas kernels for 0% -> 0%
where the time goes in v1:
time: 214 us
  waiting for transfers between devices  138 us (64%)
  other arithmetic  29.5 us (14%)
  between operations  13.5 us (6%)
  local copies, waits for them, and re-layouts  13.1 us (6%)
  starting transfers between devices  10.7 us (5%)
  matrix products  8.89 us (4%)
    psum x2, waiting for transfers between devices, from_root(): return lax.psum(kept, axis)  101 us
    ppermute x4, waiting for transfers between devices, body(): y_new = lax.ppermute(y_new, 'row', row_list)  36.7 us
    another operation x3, other arithmetic, factor(): lower_factor = jnp.linalg.cholesky(symmetric)  12.4 us
    ppermute x3, starting transfers between devices, body(): earlier = lax.ppermute(earlier, 'row', fields)  10.7 us
    another operation x1, other arithmetic, factor(): jax.scipy.linalg.solve_triangular(lower_factor, identity, lower=True)  9.81 us
    dot_general x1, matrix products, body(): lax.dot_general(panel, mirror, (((1,), (1,)), ((), ())), precision=lax.Pr...  6.97 us
  transfers between devices with their start and end apart: 9, of which 6 were waited for; matrix products, arithmetic and copies ran while one was open for 4% of the time, Pallas kernels for 0%

profile of v1, /device:TPU:0, one launch (start us, length us, event | category | flops | bytes accessed | tf_op | source)
XLA Modules:
  0.0 213.9 jit_solution(17150203559193433912)
XLA Ops:
  6.5 0.8 slice.64
  7.5 0.9 bitcast_add_fusion.1
  8.5 11.7 %cholesky.19 = f32[128,128]{1,0:T(8,128)S(1)} custom-call(f32[128,128]{1,0:T(8,128)S(1)} %fusion.4), custom_call_target="Cholesky" | custom-call | tf_op jit(solution)/shard_map/jit(cholesky)/cholesky | solution.py:16
  20.2 0.6 compare_reduce_fusion.1
  20.9 0.7 fusion.5
  21.5 9.8 %custom-call.7 = f32[1,128,128]{1,2,0:T(8,128)S(1)} custom-call(f32[1,128,128]{2,1,0:T(8,128)S(1)} %get-tuple-element.30), custom_call_target="InvertDiagBlocksLowerTriangular" | custom-call | tf_op jit(solution)/shard_map/jit(_solve_triangular)/triangular_solve | solution.py:18
  31.6 0.7 maximum_select_fusion
  32.3 57.0 %all-reduce.3.cloned.1.call-done = f32[2,128,128]{2,1,0:T(8,128)} async-done(((f32[2,128,128]{2,1,0:T(8,128)}), f32[2,128,128]{2,1,0:T(8,128)}) %all-reduce.3.cloned.1.call-update) | async-done | bytes 131088 | tf_op jit(solution)/shard_map/psum | solution.py:11
  89.3 1.7 convolution_bitcast_fusion
  91.0 0.9 fusion.2
  91.8 0.8 broadcast_select_fusion
  92.7 44.5 %all-reduce.5.cloned.1.call-done = f32[1024,128]{1,0:T(8,128)} async-done(((f32[1024,128]{1,0:T(8,128)}), f32[1024,128]{1,0:T(8,128)}) %all-reduce.5.cloned.1.call-update) | async-done | bytes 524304 | tf_op jit(solution)/shard_map/psum | solution.py:11
  137.2 3.6 %collective-permute-start.1 = (f32[1024,128]{1,0:T(8,128)}, f32[1024,128]{1,0:T(8,128)S(1)}, u32[]{:S(2)}, u32[]{:S(2)}) collective-permute-start(f32[1024,128]{1,0:T(8,128)} %all-reduce.5.cloned.1.call-done), channel_id=1, source_target_pairs={{0,28},{4,0},{8,4},{12,8},{16,12},{20,16},{24,20},{28,24},{1,29},{... | collective-permute-start | bytes 1572872 | tf_op jit(solution)/shard_map/ppermute | solution.py:55
  140.8 10.6 %collective-permute-done = f32[1024,128]{1,0:T(8,128)S(1)} collective-permute-done((f32[1024,128]{1,0:T(8,128)}, f32[1024,128]{1,0:T(8,128)S(1)}, u32[]{:S(2)}, u32[]{:S(2)}) %collective-permute-start) | collective-permute-done | bytes 524320 | tf_op jit(solution)/shard_map/ppermute | solution.py:52
  151.6 3.5 %collective-permute-start.3 = (f32[1024,128]{1,0:T(8,128)S(1)}, f32[1024,128]{1,0:T(8,128)S(1)}, u32[]{:S(2)}, u32[]{:S(2)}) collective-permute-start(f32[1024,128]{1,0:T(8,128)S(1)} %collective-permute-done.1), channel_id=1, source_target_pairs={{0,28},{4,0},{8,4},{12,8},{16,12},{20,16},{24,20},{28,24},{1,29},{... | collective-permute-start | bytes 1572872 | tf_op jit(solution)/shard_map/ppermute | solution.py:55
  155.1 12.2 %collective-permute-done.2 = f32[1024,128]{1,0:T(8,128)S(1)} collective-permute-done((f32[1024,128]{1,0:T(8,128)S(1)}, f32[1024,128]{1,0:T(8,128)S(1)}, u32[]{:S(2)}, u32[]{:S(2)}) %collective-permute-start.2) | collective-permute-done | bytes 524320 | tf_op jit(solution)/shard_map/ppermute | solution.py:52
  167.3 0.6 compare_reduce_fusion
  168.0 2.3 %broadcast_in_dim.55 = f32[8192,128]{1,0:T(8,128)} broadcast(f32[]{:T(128)} %constant.193.clone.1), dimensions={} | broadcast | bytes 4194308 | tf_op jit(solution)/shard_map/broadcast_in_dim | solution.py:46
  170.3 0.8 constant_dynamic-update-slice_fusion.7
  171.1 3.5 %collective-permute-start.5 = (f32[1024,128]{1,0:T(8,128)S(1)}, f32[1024,128]{1,0:T(8,128)S(1)}, u32[]{:S(2)}, u32[]{:S(2)}) collective-permute-start(f32[1024,128]{1,0:T(8,128)S(1)} %collective-permute-done.3), channel_id=1, source_target_pairs={{0,28},{4,0},{8,4},{12,8},{16,12},{20,16},{24,20},{28,24},{1,29},{... | collective-permute-start | bytes 1572872 | tf_op jit(solution)/shard_map/ppermute | solution.py:55
  174.7 0.8 constant_dynamic-update-slice_fusion.6
  175.5 7.6 %collective-permute-done.4 = f32[1024,128]{1,0:T(8,128)S(1)} collective-permute-done((f32[1024,128]{1,0:T(8,128)S(1)}, f32[1024,128]{1,0:T(8,128)S(1)}, u32[]{:S(2)}, u32[]{:S(2)}) %collective-permute-start.4) | collective-permute-done | bytes 524320 | tf_op jit(solution)/shard_map/ppermute | solution.py:52
  183.1 0.8 constant_dynamic-update-slice_fusion.5
  183.9 0.8 constant_dynamic-update-slice_fusion.4
  184.7 0.8 constant_dynamic-update-slice_fusion.3
  185.6 0.8 constant_dynamic-update-slice_fusion.2
  186.4 0.8 constant_dynamic-update-slice_fusion.1
  187.2 6.3 %collective-permute-done.6 = f32[1024,128]{1,0:T(8,128)S(1)} collective-permute-done((f32[1024,128]{1,0:T(8,128)S(1)}, f32[1024,128]{1,0:T(8,128)S(1)}, u32[]{:S(2)}, u32[]{:S(2)}) %collective-permute-start.6) | collective-permute-done | bytes 524320 | tf_op jit(solution)/shard_map/ppermute | solution.py:52
  193.5 0.8 constant_dynamic-update-slice_fusion
  194.3 2.8 %gather_fusion = f32[8,128,128]{2,1,0:T(8,128)S(1)} fusion(f32[64,128,128]{2,1,0:T(8,128)} %bitcast.10, s32[1024]{0:T(1024)S(1)} %pad_clamp_fusion), kind=kCustom, calls=%fused_computation | custom fusion | bytes 1048608 | tf_op jit(solution)/shard_map/jit(_take)/gather | solution.py:63
  197.7 7.0 %subtract_select_fusion = f32[1024,1024]{1,0:T(8,128)} fusion(f32[1024,1024]{1,0:T(8,128)} %param.5, pred[128,8,8,128]{3,2,1,0:T(8,128)(4,1)S(1)} %bitcast.37, f32[1024,128]{1,0:T(8,128)S(1)} %copy-done, f32[1024,128]{1,0:T(8,128)S(1)} %bitcast_select_fusion), kind=kOutput, calls=%fused_computation.1 | convolution fusion | flops 1612709888 | bytes 10485760 | tf_op jit(solution)/shard_map/dot_general | solution.py:64
  204.6 2.5 %fusion = f32[1024,1024]{1,0:T(8,128)} fusion(f32[1024,1024]{1,0:T(8,128)} %subtract_select_fusion, f32[1024,128]{1,0:T(8,128)S(1)} %copy-done, pred[]{:T(512)} %compare_reduce_fusion, pred[]{:T(512)S(6)} %eq.19), kind=kLoop, calls=%fused_computation.5 | loop fusion | flops 262144 | bytes 1573377 | tf_op jit(solution)/shard_map/scatter | solution.py:78
  (29 shorter events, 1.3 us)
Async XLA Ops:
  6.5 82.8 %all-reduce.3.cloned.1.call-start = ((), (), s32[]{:S(2)}) async-start(), calls=%async_computation | async-start | bytes 262144 | tf_op jit(solution)/shard_map/psum | solution.py:11
  32.3 104.9 %all-reduce.5.cloned.1.call-start = ((), (), s32[]{:S(2)}) async-start(), calls=%async_computation.1 | async-start | bytes 1048576 | tf_op jit(solution)/shard_map/psum | solution.py:11
  137.2 33.1 %copy-start = (f32[1024,128]{1,0:T(8,128)S(1)}, f32[1024,128]{1,0:T(8,128)}, u32[]{:S(2)}) copy-start(f32[1024,128]{1,0:T(8,128)} %all-reduce.5.cloned.1.call-done) | copy-start | bytes 1572868
  137.2 14.3 %collective-permute-start = (f32[1024,128]{1,0:T(8,128)}, f32[1024,128]{1,0:T(8,128)S(1)}, u32[]{:S(2)}, u32[]{:S(2)}) collective-permute-start(f32[1024,128]{1,0:T(8,128)} %all-reduce.5.cloned.1.call-done), channel_id=1, source_target_pairs={{0,4},{4,8},{8,12},{12,16},{16,20},{20,24},{24,28},{28,0},{1,5},{5... | collective-permute-start | bytes 1572872 | tf_op jit(solution)/shard_map/ppermute | solution.py:52
  137.2 14.3 %collective-permute-start.1 = (f32[1024,128]{1,0:T(8,128)}, f32[1024,128]{1,0:T(8,128)S(1)}, u32[]{:S(2)}, u32[]{:S(2)}) collective-permute-start(f32[1024,128]{1,0:T(8,128)} %all-reduce.5.cloned.1.call-done), channel_id=1, source_target_pairs={{0,28},{4,0},{8,4},{12,8},{16,12},{20,16},{24,20},{28,24},{1,29},{... | collective-permute-start | bytes 1572872 | tf_op jit(solution)/shard_map/ppermute | solution.py:55
  151.5 15.9 %collective-permute-start.2 = (f32[1024,128]{1,0:T(8,128)S(1)}, f32[1024,128]{1,0:T(8,128)S(1)}, u32[]{:S(2)}, u32[]{:S(2)}) collective-permute-start(f32[1024,128]{1,0:T(8,128)S(1)} %collective-permute-done), channel_id=1, source_target_pairs={{0,4},{4,8},{8,12},{12,16},{16,20},{20,24},{24,28},{28,0},{1,5},{5... | collective-permute-start | bytes 1572872 | tf_op jit(solution)/shard_map/ppermute | solution.py:52
  151.6 19.6 %collective-permute-start.3 = (f32[1024,128]{1,0:T(8,128)S(1)}, f32[1024,128]{1,0:T(8,128)S(1)}, u32[]{:S(2)}, u32[]{:S(2)}) collective-permute-start(f32[1024,128]{1,0:T(8,128)S(1)} %collective-permute-done.1), channel_id=1, source_target_pairs={{0,28},{4,0},{8,4},{12,8},{16,12},{20,16},{24,20},{28,24},{1,29},{... | collective-permute-start | bytes 1572872 | tf_op jit(solution)/shard_map/ppermute | solution.py:55
  167.3 15.8 %collective-permute-start.4 = (f32[1024,128]{1,0:T(8,128)S(1)}, f32[1024,128]{1,0:T(8,128)S(1)}, u32[]{:S(2)}, u32[]{:S(2)}) collective-permute-start(f32[1024,128]{1,0:T(8,128)S(1)} %collective-permute-done.2), channel_id=1, source_target_pairs={{0,4},{4,8},{8,12},{12,16},{16,20},{20,24},{24,28},{28,0},{1,5},{5... | collective-permute-start | bytes 1572872 | tf_op jit(solution)/shard_map/ppermute | solution.py:52
  171.1 15.3 %collective-permute-start.5 = (f32[1024,128]{1,0:T(8,128)S(1)}, f32[1024,128]{1,0:T(8,128)S(1)}, u32[]{:S(2)}, u32[]{:S(2)}) collective-permute-start(f32[1024,128]{1,0:T(8,128)S(1)} %collective-permute-done.3), channel_id=1, source_target_pairs={{0,28},{4,0},{8,4},{12,8},{16,12},{20,16},{24,20},{28,24},{1,29},{... | collective-permute-start | bytes 1572872 | tf_op jit(solution)/shard_map/ppermute | solution.py:55
  183.1 10.4 %collective-permute-start.6 = (f32[1024,128]{1,0:T(8,128)S(1)}, f32[1024,128]{1,0:T(8,128)S(1)}, u32[]{:S(2)}, u32[]{:S(2)}) collective-permute-start(f32[1024,128]{1,0:T(8,128)S(1)} %collective-permute-done.4), channel_id=1, source_target_pairs={{0,4},{4,8},{8,12},{12,16},{16,20},{20,24},{24,28},{28,0},{1,5},{5... | collective-permute-start | bytes 1572872 | tf_op jit(solution)/shard_map/ppermute | solution.py:52
Sparse Core Ops, SparseCore 0:
  32.4 56.8 all-reduce.2
  92.8 44.3 all-reduce.4
